TPU v7x, 32 devices: a whole 2x2x4 slice. The times are simulated.
32 devices in a mesh: row: 8 (over y, x, core), col: 4 (over z).
Axes of the slice: x: 2, y: 2, z: 4, core: 2. Of those that a mesh axis runs over, the one named last changes fastest.
Arguments:
- inputs: bfloat16 [32768, 261], P('row'), may hold values from -6 to 6
- latent: bfloat16 [512, 1024], P('row', 'col'), may hold values from -6 to 6
- gain_latent: float32 [1024], P('col'), may hold values from 0.25 to 1.75
- gain_inputs: float32 [261], replicated, may hold values from 0.25 to 1.75
- cross_query: bfloat16 [1024, 1024], P('col', 'row'), may hold values from -0.1875 to 0.1875
- cross_keys: bfloat16 [261, 1024], P(None, 'col'), may hold values from -0.375 to 0.375
- cross_values: bfloat16 [261, 1024], P(None, 'col'), may hold values from -0.375 to 0.375
- cross_output: bfloat16 [1024, 1024], P('col', 'row'), may hold values from -3 to 3
- cross_gain: float32 [1024], P('col'), may hold values from 0.25 to 1.75
- cross_up: bfloat16 [1024, 1024], P('row', 'col'), may hold values from -0.1875 to 0.1875
- cross_down: bfloat16 [1024, 1024], P('col', 'row'), may hold values from -0.1875 to 0.1875
- self_gain: float32 [1024], P('col'), may hold values from 0.25 to 1.75
- self_query: bfloat16 [1024, 1024], P('row', 'col'), may hold values from -0.1875 to 0.1875
- self_keys: bfloat16 [1024, 1024], P('row', 'col'), may hold values from -0.1875 to 0.1875
- self_values: bfloat16 [1024, 1024], P('row', 'col'), may hold values from -0.1875 to 0.1875
- self_output: bfloat16 [1024, 1024], P('col', 'row'), may hold values from -2 to 2
- self_mlp_gain: float32 [1024], P('col'), may hold values from 0.25 to 1.75
- self_mlp_up: bfloat16 [1024, 1024], P('row', 'col'), may hold values from -0.1875 to 0.1875
- self_mlp_down: bfloat16 [1024, 1024], P('col', 'row'), may hold values from -0.1875 to 0.1875
- cotangent: bfloat16 [16384, 1024], P('row', 'col'), may hold values from -6 to 6
Outputs:
- result: bfloat16 [16384, 1024], P('row', 'col')
- grad_inputs: float32 [32768, 261], P(('row', 'col'))
- grad_latent: float32 [512, 1024], P('row', 'col')
- grad_gain_latent: float32 [1024], P('col')
- grad_gain_inputs: float32 [261], replicated
- grad_cross_query: float32 [1024, 1024], P('col', 'row')
- grad_cross_keys: float32 [261, 1024], P(None, 'col')
- grad_cross_values: float32 [261, 1024], P(None, 'col')
- grad_cross_output: float32 [1024, 1024], P('col', 'row')
- grad_cross_gain: float32 [1024], P('col')
- grad_cross_up: float32 [1024, 1024], P('row', 'col')
- grad_cross_down: float32 [1024, 1024], P('col', 'row')
- grad_self_gain: float32 [1024], P('col')
- grad_self_query: float32 [1024, 1024], P('row', 'col')
- grad_self_keys: float32 [1024, 1024], P('row', 'col')
- grad_self_values: float32 [1024, 1024], P('row', 'col')
- grad_self_output: float32 [1024, 1024], P('col', 'row')
- grad_self_mlp_gain: float32 [1024], P('col')
- grad_self_mlp_up: float32 [1024, 1024], P('row', 'col')
- grad_self_mlp_down: float32 [1024, 1024], P('col', 'row')
All inputs are finite; a program needn't handle non-finite values.
Results may differ from a plain program's by a relative error of at most 0.039.
Values may be sent and summed in bfloat16 or wider, within the bound.
No kernel may reach another device: no remote copies, remote signals or barrier semaphores. Data moves between devices by JAX's collectives and lax.ppermute only.
A program may use at most 192 MiB of HBM per device.

v0:
```python
import jax
import jax.numpy as jnp
from jax import lax
from jax.sharding import PartitionSpec as P

HEADS = 8
M = 1024
MB = 4


epsilon = 1e-05


def for_sending(value):

    def short(part):
        return part.astype(jnp.bfloat16) if part.dtype == jnp.float32 else part

    return jax.tree.map(short, value)


def matmul_nn(left_side, right_side):
    return jnp.dot(left_side, right_side, preferred_element_type=jnp.float32)


def matmul_nt(left_side, right_side):
    return lax.dot_general(
        left_side, right_side, (((1,), (1,)), ((), ())), preferred_element_type=jnp.float32
    )


def matmul_tn(left_side, right_side):
    return lax.dot_general(
        left_side, right_side, (((0,), (0,)), ((), ())), preferred_element_type=jnp.float32
    )


def row_stats(first_term, second_term):
    return lax.psum((jnp.sum(first_term, axis=-1), jnp.sum(second_term, axis=-1)), "col")


def norm_forward(values, gain, full_width):
    row_total, row_squares = row_stats(values, values * values)
    average = row_total / full_width
    spread = row_squares / full_width - average * average
    inv_scale = lax.rsqrt(spread + epsilon)[:, None]
    normed = (values - average[:, None]) * inv_scale
    return (normed * gain, normed, inv_scale)


def norm_backward(upstream, gain, normed, inv_scale, full_width):
    scaled = upstream * gain
    first_sum, second_sum = row_stats(scaled, scaled * normed)
    back_rows = inv_scale * (
        scaled - first_sum[:, None] / full_width - normed * (second_sum[:, None] / full_width)
    )
    return (back_rows, jnp.sum(upstream * normed, axis=0))


def input_norm(values, gain):
    average = jnp.mean(values, axis=-1, keepdims=True)
    centred = values - average
    inv_scale = lax.rsqrt(jnp.mean(centred * centred, axis=-1, keepdims=True) + epsilon)
    normed = centred * inv_scale
    return (normed * gain, normed, inv_scale)


def gelu_value(values):
    return jax.nn.gelu(values, approximate=True)


def gelu_grad(values, upstream):
    return jax.vjp(gelu_value, values)[1](upstream)[0]


def softmax_rows(scores):
    peak_value = jnp.max(scores, axis=-1, keepdims=True)
    exponent = jnp.exp(scores - peak_value)
    row_total = jnp.sum(exponent, axis=-1, keepdims=True)
    return (exponent / row_total, peak_value + jnp.log(row_total))


def softmax_back(soft_scores, upstream):
    return soft_scores * (upstream - jnp.sum(upstream * soft_scores, axis=-1, keepdims=True))


def widen(values):
    return lax.all_gather(values, "col", axis=1, tiled=True)


def narrow(values):
    return lax.psum_scatter(
        values.astype(jnp.bfloat16), "col", scatter_dimension=1, tiled=True
    ).astype(jnp.float32)


def widen_grad(values):
    return lax.all_gather(values, "col", axis=1, tiled=True)


def narrow_grad(values):
    return lax.psum_scatter(
        values.astype(jnp.bfloat16), "col", scatter_dimension=1, tiled=True
    ).astype(jnp.float32)


def reduce_cols(grads):
    return jax.tree.map(
        lambda part: part.astype(jnp.float32),
        lax.psum_scatter(for_sending(grads), "row", scatter_dimension=1, tiled=True),
    )


def forward_sum(left_low, weight_whole):
    return narrow(matmul_nn(left_low, weight_whole))


def backward_sum(grad_list, weight_list):
    total = matmul_nt(grad_list[0], weight_list[0])
    for index in range(1, len(grad_list)):
        total = total + matmul_nt(grad_list[index], weight_list[index])
    return narrow_grad(total)


def local(
    inputs,
    latent,
    gain_latent,
    gain_inputs,
    cross_query,
    cross_keys,
    cross_values,
    cross_output,
    cross_gain,
    cross_up,
    cross_down,
    self_gain,
    self_query,
    self_keys,
    self_values,
    self_output,
    self_mlp_gain,
    self_mlp_up,
    self_mlp_down,
    cotangent,
):
    col_count = lax.axis_size("col")
    row_count = lax.axis_size("row")
    local_width = latent.shape[1]
    full_width = local_width * col_count
    heads_here = HEADS // col_count
    head_size = full_width // HEADS
    lat_count = latent.shape[0] * row_count
    in_rows = inputs.shape[0] // MB
    out_rows = cotangent.shape[0] // MB
    images = out_rows // lat_count
    in_width = inputs.shape[1]
    cross_scale = full_width ** (-0.5)
    self_scale = head_size ** (-0.5)
    bf_type = jnp.bfloat16
    float_kind = jnp.float32
    col_shape = (local_width, full_width)
    col_total = tuple((jnp.zeros(col_shape, float_kind) for index in range(5)))
    row_total = tuple((jnp.zeros((full_width, local_width), float_kind) for index in range(5)))
    sum_cross_keys = jnp.zeros((in_width, local_width), float_kind)
    sum_cross_values = jnp.zeros((in_width, local_width), float_kind)
    lat_resid = jnp.zeros((lat_count, local_width), float_kind)
    lat_norm_grad = jnp.zeros((lat_count, local_width), float_kind)
    gain_sums = tuple((jnp.zeros((local_width,), float_kind) for index in range(3)))
    gain_pix = jnp.zeros((in_width,), float_kind)
    results = []
    pix_grads = []
    for micro_batch in range(MB):
        lat_all, cross_up_all, self_query_all, self_keys_all, self_values_all, self_up_all = (
            lax.all_gather(latent, "row", axis=0, tiled=True),
            lax.all_gather(cross_up, "row", axis=0, tiled=True),
            lax.all_gather(self_query, "row", axis=0, tiled=True),
            lax.all_gather(self_keys, "row", axis=0, tiled=True),
            lax.all_gather(self_values, "row", axis=0, tiled=True),
            lax.all_gather(self_mlp_up, "row", axis=0, tiled=True),
        )
        cross_query_all, cross_output_all, cross_down_all, self_output_all, self_down_all = (
            lax.all_gather(cross_query, "row", axis=1, tiled=True),
            lax.all_gather(cross_output, "row", axis=1, tiled=True),
            lax.all_gather(cross_down, "row", axis=1, tiled=True),
            lax.all_gather(self_output, "row", axis=1, tiled=True),
            lax.all_gather(self_mlp_down, "row", axis=1, tiled=True),
        )
        lat_value = lat_all.astype(float_kind)
        lat_normed, lat_hat, lat_scale = norm_forward(lat_value, gain_latent, full_width)
        lat_low = lat_normed.astype(bf_type)
        query_rows = forward_sum(lat_low, cross_query_all).astype(bf_type)
        pixels = inputs[micro_batch * in_rows : (micro_batch + 1) * in_rows].astype(float_kind)
        pix_normed, pix_hat, pix_scale = input_norm(pixels, gain_inputs)
        pix_low = pix_normed.astype(bf_type)
        key_rows = matmul_nn(pix_low, cross_keys).astype(bf_type)
        values = matmul_nn(pix_low, cross_values).astype(bf_type)
        key_image_rows = key_rows.reshape(images, M, local_width)
        value_image_rows = values.reshape(images, M, local_width)
        partial_scores = jnp.einsum(
            "iw,lyw->liy", query_rows, key_image_rows, preferred_element_type=float_kind
        )
        scores = (
            lax.psum(partial_scores.astype(jnp.bfloat16), "col").astype(jnp.float32) * cross_scale
        )
        soft_scores, cross_lse = softmax_rows(scores)
        softmax_reduced = soft_scores.astype(bf_type)
        attended = (
            jnp.einsum(
                "czv,cvj->czj", softmax_reduced, value_image_rows, preferred_element_type=float_kind
            )
            .astype(bf_type)
            .reshape(out_rows, local_width)
        )
        cross_term = forward_sum(attended, cross_output_all)
        state_one = (cross_term.reshape(images, lat_count, local_width) + lat_value).reshape(
            out_rows, local_width
        )
        mlp_in, mlp_hat, mlp_scale = norm_forward(state_one, cross_gain, full_width)
        mlp_wide = widen(mlp_in.astype(bf_type))
        hidden_one = matmul_nn(mlp_wide, cross_up_all)
        active_one = gelu_value(hidden_one).astype(bf_type)
        state_two = state_one + forward_sum(active_one, cross_down_all)
        attn_in, attn_hat, attn_scale = norm_forward(state_two, self_gain, full_width)
        attn_wide = widen(attn_in.astype(bf_type))
        head_shape = (images, lat_count, heads_here, head_size)
        head_q = matmul_nn(attn_wide, self_query_all).astype(bf_type).reshape(head_shape)
        head_k = matmul_nn(attn_wide, self_keys_all).astype(bf_type).reshape(head_shape)
        head_v = matmul_nn(attn_wide, self_values_all).astype(bf_type).reshape(head_shape)
        self_scores = (
            jnp.einsum("bqhd,bkhd->bhqk", head_q, head_k, preferred_element_type=float_kind)
            * self_scale
        )
        self_soft, self_lse = softmax_rows(self_scores)
        self_att = (
            jnp.einsum(
                "bhqk,bkhd->bqhd",
                self_soft.astype(bf_type),
                head_v,
                preferred_element_type=float_kind,
            )
            .astype(bf_type)
            .reshape(out_rows, local_width)
        )
        state_three = state_two + forward_sum(self_att, self_output_all)
        last_in, last_hat, last_scale = norm_forward(state_three, self_mlp_gain, full_width)
        last_wide = widen(last_in.astype(bf_type))
        hidden_two = matmul_nn(last_wide, self_up_all)
        active_two = gelu_value(hidden_two).astype(bf_type)
        outputs = state_three + forward_sum(active_two, self_down_all)
        results.append(outputs.astype(bf_type))
        grad_out = cotangent[micro_batch * out_rows : (micro_batch + 1) * out_rows].astype(
            float_kind
        )
        grad_wide = widen_grad(grad_out.astype(bf_type))
        sum_self_down = matmul_tn(active_two, grad_wide)
        grad_hidden_two = gelu_grad(hidden_two, matmul_nt(grad_wide, self_down_all)).astype(bf_type)
        sum_self_up = matmul_tn(last_wide, grad_hidden_two)
        grad_last, gain_last = norm_backward(
            backward_sum((grad_hidden_two,), (self_up_all,)),
            self_mlp_gain,
            last_hat,
            last_scale,
            full_width,
        )
        grad_three = grad_out + grad_last
        grad_three_wide = widen_grad(grad_three.astype(bf_type))
        sum_self_output = matmul_tn(self_att, grad_three_wide)
        grad_att = matmul_nt(grad_three_wide, self_output_all).astype(bf_type).reshape(head_shape)
        redo_scores = (
            jnp.einsum("bqhd,bkhd->bhqk", head_q, head_k, preferred_element_type=float_kind)
            * self_scale
        )
        redo_soft = jnp.exp(redo_scores - self_lse)
        grad_soft = jnp.einsum(
            "bqhd,bkhd->bhqk", grad_att, head_v, preferred_element_type=float_kind
        )
        grad_self_scores = softmax_back(redo_soft, grad_soft).astype(bf_type)
        grad_hq = (
            (
                jnp.einsum(
                    "bhqk,bkhd->bqhd", grad_self_scores, head_k, preferred_element_type=float_kind
                )
                * self_scale
            )
            .astype(bf_type)
            .reshape(out_rows, local_width)
        )
        grad_hk = (
            (
                jnp.einsum(
                    "bhqk,bqhd->bkhd", grad_self_scores, head_q, preferred_element_type=float_kind
                )
                * self_scale
            )
            .astype(bf_type)
            .reshape(out_rows, local_width)
        )
        grad_hv = (
            jnp.einsum(
                "bhqk,bqhd->bkhd",
                redo_soft.astype(bf_type),
                grad_att,
                preferred_element_type=float_kind,
            )
            .astype(bf_type)
            .reshape(out_rows, local_width)
        )
        sum_self_query = matmul_tn(attn_wide, grad_hq)
        sum_self_keys = matmul_tn(attn_wide, grad_hk)
        sum_self_values = matmul_tn(attn_wide, grad_hv)
        grad_attn_in = backward_sum(
            (grad_hq, grad_hk, grad_hv), (self_query_all, self_keys_all, self_values_all)
        )
        grad_mid, gain_attn = norm_backward(
            grad_attn_in, self_gain, attn_hat, attn_scale, full_width
        )
        grad_two = grad_three + grad_mid
        grad_two_wide = widen_grad(grad_two.astype(bf_type))
        sum_cross_down = matmul_tn(active_one, grad_two_wide)
        grad_hidden_one = gelu_grad(hidden_one, matmul_nt(grad_two_wide, cross_down_all)).astype(
            bf_type
        )
        sum_cross_up = matmul_tn(mlp_wide, grad_hidden_one)
        grad_mlp, gain_mlp = norm_backward(
            backward_sum((grad_hidden_one,), (cross_up_all,)),
            cross_gain,
            mlp_hat,
            mlp_scale,
            full_width,
        )
        grad_one = grad_two + grad_mlp
        lat_resid = lat_resid + jnp.sum(grad_one.reshape(images, lat_count, local_width), axis=0)
        grad_one_wide = widen_grad(grad_one.astype(bf_type))
        sum_cross_output = matmul_tn(attended, grad_one_wide)
        gradient_attended_rows = (
            matmul_nt(grad_one_wide, cross_output_all)
            .astype(bf_type)
            .reshape(images, lat_count, local_width)
        )
        partial_grad = jnp.einsum(
            "pex,plx->pel",
            gradient_attended_rows,
            value_image_rows,
            preferred_element_type=float_kind,
        )
        grad_cross_soft = lax.psum(partial_grad.astype(jnp.bfloat16), "col").astype(jnp.float32)
        gradient_cross_logits = softmax_back(soft_scores, grad_cross_soft).astype(bf_type)
        grad_queries = (
            (
                jnp.einsum(
                    "czv,cvj->czj",
                    gradient_cross_logits,
                    key_image_rows,
                    preferred_element_type=float_kind,
                )
                * cross_scale
            )
            .astype(bf_type)
            .reshape(out_rows, local_width)
        )
        grad_keys = (
            (
                jnp.einsum(
                    "hnm,nq->hmq",
                    gradient_cross_logits,
                    query_rows,
                    preferred_element_type=float_kind,
                )
                * cross_scale
            )
            .astype(bf_type)
            .reshape(in_rows, local_width)
        )
        grad_values = (
            jnp.einsum(
                "awg,awy->agy",
                softmax_reduced,
                gradient_attended_rows,
                preferred_element_type=float_kind,
            )
            .astype(bf_type)
            .reshape(in_rows, local_width)
        )
        sum_cross_keys = sum_cross_keys + matmul_tn(pix_low, grad_keys)
        sum_cross_values = sum_cross_values + matmul_tn(pix_low, grad_values)
        grad_pix = matmul_nt(grad_keys, cross_keys) + matmul_nt(grad_values, cross_values)
        gain_pix = gain_pix + jnp.sum(grad_pix * pix_hat, axis=0)
        scaled_pix = grad_pix * gain_inputs
        pix_grads.append(
            pix_scale
            * (
                scaled_pix
                - jnp.mean(scaled_pix, axis=-1, keepdims=True)
                - pix_hat * jnp.mean(scaled_pix * pix_hat, axis=-1, keepdims=True)
            )
        )
        grad_query_wide = widen_grad(grad_queries)
        sum_cross_query = matmul_tn(jnp.tile(lat_low, (images, 1)), grad_query_wide)
        lat_norm_grad = lat_norm_grad + jnp.sum(
            matmul_nt(grad_query_wide, cross_query_all).reshape(images, lat_count, local_width),
            axis=0,
        )
        row_total = tuple(
            (
                total + term
                for total, term in zip(
                    row_total,
                    (sum_cross_up, sum_self_query, sum_self_keys, sum_self_values, sum_self_up),
                )
            )
        )
        gain_sums = tuple(
            (total + term for total, term in zip(gain_sums, (gain_mlp, gain_attn, gain_last)))
        )
        batch_cols = (
            sum_cross_query,
            sum_cross_output,
            sum_cross_down,
            sum_self_output,
            sum_self_down,
        )
        col_total = tuple((total + term for total, term in zip(col_total, batch_cols)))
    col_total = reduce_cols(col_total)
    lat_back, gain_lat = norm_backward(lat_norm_grad, gain_latent, lat_hat, lat_scale, full_width)
    row_shares = jax.tree.map(
        lambda part: part.astype(jnp.float32),
        lax.psum_scatter(
            for_sending((lat_resid + lat_back,) + row_total), "row", scatter_dimension=0, tiled=True
        ),
    )
    pix_total, pix_gain = (
        lax.psum_scatter(
            jnp.concatenate(pix_grads, axis=0).astype(jnp.bfloat16),
            "col",
            scatter_dimension=0,
            tiled=True,
        ).astype(jnp.float32),
        lax.psum_scatter(
            jnp.broadcast_to(gain_pix[None, :], (col_count, in_width)).astype(jnp.bfloat16),
            "col",
            scatter_dimension=0,
            tiled=True,
        ).astype(jnp.float32),
    )
    small_sums = (
        lax.psum(gain_lat.astype(jnp.bfloat16), "row").astype(jnp.float32),
        lax.psum(pix_gain[0].astype(jnp.bfloat16), "row").astype(jnp.float32),
        lax.psum(gain_sums[0].astype(jnp.bfloat16), "row").astype(jnp.float32),
        lax.psum(gain_sums[1].astype(jnp.bfloat16), "row").astype(jnp.float32),
        lax.psum(gain_sums[2].astype(jnp.bfloat16), "row").astype(jnp.float32),
        lax.psum(sum_cross_keys.astype(jnp.bfloat16), "row").astype(jnp.float32),
        lax.psum(sum_cross_values.astype(jnp.bfloat16), "row").astype(jnp.float32),
    )
    (
        grad_lat_gain,
        grad_pix_gain,
        grad_cross_gain,
        grad_self_gain,
        grad_mlp_gain,
        grad_cross_keys,
        grad_cross_values,
    ) = small_sums
    grad_latent, grad_cross_up, grad_self_query, grad_self_keys, grad_self_values, grad_self_up = (
        row_shares
    )
    grad_cross_query, grad_cross_output, grad_cross_down, grad_self_output, grad_self_down = (
        col_total
    )
    return (
        jnp.concatenate(results, axis=0),
        pix_total,
        grad_latent,
        grad_lat_gain,
        grad_pix_gain,
        grad_cross_query,
        grad_cross_keys,
        grad_cross_values,
        grad_cross_output,
        grad_cross_gain,
        grad_cross_up,
        grad_cross_down,
        grad_self_gain,
        grad_self_query,
        grad_self_keys,
        grad_self_values,
        grad_self_output,
        grad_mlp_gain,
        grad_self_up,
        grad_self_down,
    )


def solution(mesh):
    return jax.shard_map(
        local,
        mesh=mesh,
        in_specs=(
            P("row", None),
            P("row", "col"),
            P("col"),
            P(),
            P("col", "row"),
            P(None, "col"),
            P(None, "col"),
            P("col", "row"),
            P("col"),
            P("row", "col"),
            P("col", "row"),
            P("col"),
            P("row", "col"),
            P("row", "col"),
            P("row", "col"),
            P("col", "row"),
            P("col"),
            P("row", "col"),
            P("col", "row"),
            P("row", "col"),
        ),
        out_specs=(
            P("row", "col"),
            P(("row", "col"), None),
            P("row", "col"),
            P("col"),
            P(),
            P("col", "row"),
            P(None, "col"),
            P(None, "col"),
            P("col", "row"),
            P("col"),
            P("row", "col"),
            P("col", "row"),
            P("col"),
            P("row", "col"),
            P("row", "col"),
            P("row", "col"),
            P("col", "row"),
            P("col"),
            P("row", "col"),
            P("col", "row"),
        ),
        check_vma=False,
    )
```

profile of v0, /device:TPU:0, one launch (start us, length us, event | category | flops | bytes accessed | tf_op | source)
XLA Modules:
  0.0 2879.6 jit_solution(14776914867968977477)
XLA Ops:
  81.9 39.1 %all-reduce.25.cloned.1.call-done = bf16[1,512,1024]{1,2,0:T(8,128)(2,1)} async-done(((bf16[1,512,1024]{1,2,0:T(8,128)(2,1)}), bf16[1,512,1024]{1,2,0:T(8,128)(2,1)}) %all-reduce.25.cloned.1.call-update) | async-done | bytes 1048592 | tf_op jit(solution)/shard_map/psum | solution.py:204
  509.6 28.8 all-gather.77.cloned.1.call-done
  581.8 28.8 all-gather.79.cloned.1.call-done
  619.7 45.3 %all-reduce.27.cloned.1.call-done = bf16[1,512,1024]{1,2,0:T(8,128)(2,1)} async-done(((bf16[1,512,1024]{1,2,0:T(8,128)(2,1)}), bf16[1,512,1024]{1,2,0:T(8,128)(2,1)}) %all-reduce.27.cloned.1.call-update) | async-done | bytes 1048592 | tf_op jit(solution)/shard_map/psum | solution.py:347
  681.4 118.6 %all-reduce.33.cloned.1.call-done = (bf16[1,512,1024]{1,2,0:T(8,128)(2,1)}, bf16[1,512,1024]{1,2,0:T(8,128)(2,1)}, bf16[1,512,1024]{1,2,0:T(8,128)(2,1)}) async-done(((bf16[1,512,1024]{1,2,0:T(8,128)(2,1)}, bf16[1,512,1024]{1,2,0:T(8,128)(2,1)}, bf16[1,512,1024]{1,2,0:T(8,128)(2,1)}), (bf16[1,512,1024]{1,2,0:T(8,128)(2,1)}, bf16[1,512,1024]{1,2,0:T(8,128)(2,1)}, ...) | async-done | bytes 3145744 | tf_op jit(solution)/shard_map/psum | solution.py:204
  860.7 28.7 reduce-scatter.54.cloned.1.call-done
  1519.6 28.7 reduce-scatter.92.cloned.1.call-done
  1576.6 28.2 reduce-scatter.84.cloned.1.call-done
  1750.8 28.1 reduce-scatter.94.cloned.1.call-done
  1778.9 28.5 reduce-scatter.88.cloned.1.call-done
  1946.5 28.1 reduce-scatter.96.cloned.1.call-done
  1974.7 28.1 reduce-scatter.90.cloned.1.call-done
  2117.4 119.1 %all-reduce.31.cloned.1.call-done = (bf16[1,512,1024]{1,2,0:T(8,128)(2,1)}, bf16[1,512,1024]{1,2,0:T(8,128)(2,1)}, bf16[1,512,1024]{1,2,0:T(8,128)(2,1)}) async-done(((bf16[1,512,1024]{1,2,0:T(8,128)(2,1)}, bf16[1,512,1024]{1,2,0:T(8,128)(2,1)}, bf16[1,512,1024]{1,2,0:T(8,128)(2,1)}), (bf16[1,512,1024]{1,2,0:T(8,128)(2,1)}, bf16[1,512,1024]{1,2,0:T(8,128)(2,1)}, ...) | async-done | bytes 3145744 | tf_op jit(solution)/shard_map/psum | solution.py:347
  2396.7 35.4 %reduce-scatter.122.cloned.1.call-done = bf16[128,256]{1,0:T(8,128)(2,1)} async-done(((bf16[1024,256]{1,0:T(8,128)(2,1)}), bf16[128,256]{1,0:T(8,128)(2,1)}) %reduce-scatter.122.cloned.1.call-update) | async-done | bytes 65552 | tf_op jit(solution)/shard_map/reduce_scatter | solution.py:428
  2434.7 34.6 %reduce-scatter.130.cloned.1.call-done = bf16[128,256]{1,0:T(8,128)(2,1)} async-done(((bf16[1024,256]{1,0:T(8,128)(2,1)}), bf16[128,256]{1,0:T(8,128)(2,1)}) %reduce-scatter.130.cloned.1.call-update) | async-done | bytes 65552
  2470.9 35.6 %reduce-scatter.120.cloned.1.call-done = bf16[128,256]{1,0:T(8,128)(2,1)} async-done(((bf16[1024,256]{1,0:T(8,128)(2,1)}), bf16[128,256]{1,0:T(8,128)(2,1)}) %reduce-scatter.120.cloned.1.call-update) | async-done | bytes 65552 | tf_op jit(solution)/shard_map/reduce_scatter | solution.py:428
  2508.0 35.6 %reduce-scatter.116.cloned.1.call-done = bf16[128,256]{1,0:T(8,128)(2,1)} async-done(((bf16[1024,256]{1,0:T(8,128)(2,1)}), bf16[128,256]{1,0:T(8,128)(2,1)}) %reduce-scatter.116.cloned.1.call-update) | async-done | bytes 65552 | tf_op jit(solution)/shard_map/reduce_scatter | solution.py:428
  2545.0 35.7 %reduce-scatter.118.cloned.1.call-done = bf16[128,256]{1,0:T(8,128)(2,1)} async-done(((bf16[1024,256]{1,0:T(8,128)(2,1)}), bf16[128,256]{1,0:T(8,128)(2,1)}) %reduce-scatter.118.cloned.1.call-update) | async-done | bytes 65552 | tf_op jit(solution)/shard_map/reduce_scatter | solution.py:428
  2582.3 35.5 %reduce-scatter.128.cloned.1.call-done = bf16[128,256]{1,0:T(8,128)(2,1)} async-done(((bf16[1024,256]{1,0:T(8,128)(2,1)}), bf16[128,256]{1,0:T(8,128)(2,1)}) %reduce-scatter.128.cloned.1.call-update) | async-done | bytes 65552
  2619.5 35.4 %reduce-scatter.114.cloned.1.call-done = bf16[128,256]{1,0:T(8,128)(2,1)} async-done(((bf16[1024,256]{1,0:T(8,128)(2,1)}), bf16[128,256]{1,0:T(8,128)(2,1)}) %reduce-scatter.114.cloned.1.call-update) | async-done | bytes 65552 | tf_op jit(solution)/shard_map/reduce_scatter | solution.py:428
  2656.4 35.5 %reduce-scatter.126.cloned.1.call-done = bf16[128,256]{1,0:T(8,128)(2,1)} async-done(((bf16[1024,256]{1,0:T(8,128)(2,1)}), bf16[128,256]{1,0:T(8,128)(2,1)}) %reduce-scatter.126.cloned.1.call-update) | async-done | bytes 65552
  2706.0 42.7 %all-reduce.29.cloned.1.call-done = (bf16[261,256]{1,0:T(8,128)(2,1)}, bf16[261,256]{1,0:T(8,128)(2,1)}) async-done(((bf16[261,256]{1,0:T(8,128)(2,1)}, bf16[261,256]{1,0:T(8,128)(2,1)}), (bf16[261,256]{1,0:T(8,128)(2,1)}, bf16[261,256]{1,0:T(8,128)(2,1)})) %all-reduce.29.cloned.1.call-update) | async-done | bytes 267280 | tf_op jit(solution)/shard_map/psum | solution.py:452
  2787.3 35.8 %reduce-scatter.124.cloned.1.call-done = bf16[128,256]{1,0:T(8,128)(2,1)} async-done(((bf16[1024,256]{1,0:T(8,128)(2,1)}), bf16[128,256]{1,0:T(8,128)(2,1)}) %reduce-scatter.124.cloned.1.call-update) | async-done | bytes 65552
  2824.8 45.4 %reduce-scatter.110.cloned.1.call-done = bf16[1024,261]{0,1:T(8,128)(2,1)} async-done(((bf16[4096,261]{0,1:T(8,128)(2,1)}), bf16[1024,261]{0,1:T(8,128)(2,1)}) %reduce-scatter.110.cloned.1.call-update) | async-done | bytes 534544 | tf_op jit(solution)/shard_map/reduce_scatter | solution.py:433
  (1300 shorter events, 1874.4 us)
Async XLA Ops:
  614.7 185.4 %all-reduce.33.cloned.1.call-start = ((), (), s32[]{:S(2)}) async-start(), calls=%async_computation.118 | async-start | bytes 6291456 | tf_op jit(solution)/shard_map/psum | solution.py:204
  679.5 153.2 %reduce-scatter.78.cloned.1.call-start = ((), (), s32[]{:S(2)}) async-start(), calls=%async_computation.64 | async-start | bytes 1310720 | tf_op jit(solution)/shard_map/reduce_scatter | solution.py:92
  817.3 120.8 %all-gather.33.cloned.1.call-start = ((), (), s32[]{:S(2)}) async-start(), calls=%async_computation.43 | async-start | bytes 1310720 | tf_op jit(solution)/shard_map/all_gather | solution.py:88
  1001.6 134.0 %all-gather.35.cloned.1.call-start = ((), (), s32[]{:S(2)}) async-start(), calls=%async_computation.45 | async-start | bytes 1310720 | tf_op jit(solution)/shard_map/all_gather | solution.py:88
  1204.4 135.9 %all-gather.37.cloned.1.call-start = ((), (), s32[]{:S(2)}) async-start(), calls=%async_computation.47 | async-start | bytes 1310720 | tf_op jit(solution)/shard_map/all_gather | solution.py:88
  1376.0 143.6 %reduce-scatter.104.cloned.1.call-start = ((), (), s32[]{:S(2)}) async-start(), calls=%async_computation.94 | async-start | bytes 1310720 | tf_op jit(solution)/shard_map/reduce_scatter | solution.py:102
  1502.4 130.2 %reduce-scatter.68.cloned.1.call-start = ((), (), s32[]{:S(2)}) async-start(), calls=%async_computation.55 | async-start | bytes 1310720 | tf_op jit(solution)/shard_map/reduce_scatter | solution.py:92
  1505.2 157.9 %all-gather.83.cloned.1.call-start = ((), (), s32[]{:S(2)}) async-start(), calls=%async_computation.95 | async-start | bytes 1310720 | tf_op jit(solution)/shard_map/all_gather | solution.py:98
  1921.5 130.9 %all-gather.71.cloned.1.call-start = ((), (), s32[]{:S(2)}) async-start(), calls=%async_computation.84 | async-start | bytes 1310720 | tf_op jit(solution)/shard_map/all_gather | solution.py:98
  2027.8 208.7 %all-reduce.31.cloned.1.call-start = ((), (), s32[]{:S(2)}) async-start(), calls=%async_computation.117 | async-start | bytes 6291456 | tf_op jit(solution)/shard_map/psum | solution.py:347
  2117.0 210.5 %all-gather.89.cloned.1.call-start = ((), (), s32[]{:S(2)}) async-start(), calls=%async_computation.101 | async-start | bytes 1310720 | tf_op jit(solution)/shard_map/all_gather | solution.py:98
  2254.1 141.0 %reduce-scatter.132.cloned.1.call-start = ((), (), s32[]{:S(2)}) async-start(), calls=%async_computation.115 | async-start | bytes 589824
  2261.5 170.6 %reduce-scatter.122.cloned.1.call-start = ((), (), s32[]{:S(2)}) async-start(), calls=%async_computation.110 | async-start | bytes 589824 | tf_op jit(solution)/shard_map/reduce_scatter | solution.py:428
  2266.3 203.0 %reduce-scatter.130.cloned.1.call-start = ((), (), s32[]{:S(2)}) async-start(), calls=%async_computation.114 | async-start | bytes 589824
  2271.8 234.7 %reduce-scatter.120.cloned.1.call-start = ((), (), s32[]{:S(2)}) async-start(), calls=%async_computation.109 | async-start | bytes 589824 | tf_op jit(solution)/shard_map/reduce_scatter | solution.py:428
  2276.6 266.9 %reduce-scatter.116.cloned.1.call-start = ((), (), s32[]{:S(2)}) async-start(), calls=%async_computation.107 | async-start | bytes 589824 | tf_op jit(solution)/shard_map/reduce_scatter | solution.py:428
  2281.7 299.0 %reduce-scatter.118.cloned.1.call-start = ((), (), s32[]{:S(2)}) async-start(), calls=%async_computation.108 | async-start | bytes 589824 | tf_op jit(solution)/shard_map/reduce_scatter | solution.py:428
  2286.9 331.0 %reduce-scatter.128.cloned.1.call-start = ((), (), s32[]{:S(2)}) async-start(), calls=%async_computation.113 | async-start | bytes 589824
  2293.2 361.7 %reduce-scatter.114.cloned.1.call-start = ((), (), s32[]{:S(2)}) async-start(), calls=%async_computation.106 | async-start | bytes 589824 | tf_op jit(solution)/shard_map/reduce_scatter | solution.py:428
  2297.7 394.3 %reduce-scatter.126.cloned.1.call-start = ((), (), s32[]{:S(2)}) async-start(), calls=%async_computation.112 | async-start | bytes 589824
  2310.0 438.7 %all-reduce.29.cloned.1.call-start = ((), (), s32[]{:S(2)}) async-start(), calls=%async_computation.116 | async-start | bytes 540672 | tf_op jit(solution)/shard_map/psum | solution.py:452
  2322.7 463.2 %reduce-scatter.112.cloned.1.call-start = ((), (), s32[]{:S(2)}) async-start(), calls=%async_computation.105 | async-start | bytes 294912 | tf_op jit(solution)/shard_map/reduce_scatter | solution.py:428
  2376.1 447.1 %reduce-scatter.124.cloned.1.call-start = ((), (), s32[]{:S(2)}) async-start(), calls=%async_computation.111 | async-start | bytes 589824
  2383.6 486.6 %reduce-scatter.110.cloned.1.call-start = ((), (), s32[]{:S(2)}) async-start(), calls=%async_computation.100 | async-start | bytes 2703360 | tf_op jit(solution)/shard_map/reduce_scatter | solution.py:433
  (413 other events, 11608.9 us)
Sparse Core Ops, SparseCore 0:
  70.5 50.3 all-reduce.24
  166.4 28.6 all-gather.44
  235.6 28.6 all-gather.46
  431.6 28.4 all-gather.74
  509.7 28.6 all-gather.76
  581.9 28.6 all-gather.78
  614.8 50.1 all-reduce.26
  679.6 120.3 all-reduce.32
  1281.9 28.5 all-gather.56
  2117.1 119.3 all-reduce.30
  2241.5 28.9 all-gather.88
  2362.6 32.4 reduce-scatter.131
  2397.9 34.0 reduce-scatter.121
  2435.2 34.0 reduce-scatter.129
  2472.3 34.0 reduce-scatter.119
  2509.4 34.0 reduce-scatter.115
  2546.6 34.0 reduce-scatter.117
  2583.7 34.0 reduce-scatter.127
  2620.8 34.0 reduce-scatter.113
  2657.8 34.0 reduce-scatter.125
  2695.7 52.9 all-reduce.28
  2751.6 34.3 reduce-scatter.111
  2789.0 34.0 reduce-scatter.123
  2825.4 44.6 reduce-scatter.109
  (54 shorter events, 1447.9 us)
where the time goes:
time: 2890 us; the launch traced here: 2880 us
  waiting for transfers between devices  2080 us (72%)
  blocking collectives  321 us (11%)
  matrix products  240 us (8%)
  other arithmetic  152 us (5%)
  local copies, waits for them, and re-layouts  60.7 us (2%)
    all_gather x20, waiting for transfers between devices, widen_grad(): return lax.all_gather(values, 'col', axis=1, tiled=True)  386 us
    reduce_scatter x17, waiting for transfers between devices, narrow(): lax.psum_scatter(values.astype(jnp.bfloat16), 'col', scatter_dimension=1,...  386 us
    reduce_scatter x12, waiting for transfers between devices, narrow_grad(): lax.psum_scatter(values.astype(jnp.bfloat16), 'col', scatter_dimension=1,...  289 us
    all_gather x12, waiting for transfers between devices, widen(): return lax.all_gather(values, 'col', axis=1, tiled=True)  258 us
    reduce_scatter x6, waiting for transfers between devices, local(): lax.psum_scatter(for_sending((lat_resid + lat_back,) + row_total), 'row',...  196 us
    psum x14, blocking collectives, row_stats(): lax.psum((jnp.sum(first_term, axis=-1), jnp.sum(second_term, axis=-1)), '...  185 us
    psum x2, waiting for transfers between devices, local(): lax.psum(partial_grad.astype(jnp.bfloat16), 'col').astype(jnp.float32)  164 us
    psum x2, waiting for transfers between devices, local(): lax.psum(partial_scores.astype(jnp.bfloat16), 'col').astype(jnp.float32)  158 us
  transfers between devices with their start and end apart: 78, of which 73 were waited for; matrix products, arithmetic and copies ran while one was open for 10% of the time, Pallas kernels for 0%

commit v1 on v0

v1 whole, which is shorter than its diff:
```python
import jax
import jax.numpy as jnp
from jax import lax
from jax.sharding import PartitionSpec as P

HEADS = 8
M = 1024
EPSILON = 1e-05
BF = jnp.bfloat16
F32 = jnp.float32
BOTH = ("row", "col")


def nn(left, right):
    return lax.dot_general(left, right, (((1,), (0,)), ((), ())), preferred_element_type=F32)


def nt(left, right):
    return lax.dot_general(left, right, (((1,), (1,)), ((), ())), preferred_element_type=F32)


def tn(left, right):
    return lax.dot_general(left, right, (((0,), (0,)), ((), ())), preferred_element_type=F32)


def norm(values, gain):
    average = jnp.mean(values, axis=-1, keepdims=True)
    centred = values - average
    scale = lax.rsqrt(jnp.mean(centred * centred, axis=-1, keepdims=True) + EPSILON)
    hat = centred * scale
    return (hat * gain).astype(BF), hat, scale


def norm_back(upstream, gain, hat, scale):
    scaled = upstream * gain
    first = jnp.mean(scaled, axis=-1, keepdims=True)
    second = jnp.mean(scaled * hat, axis=-1, keepdims=True)
    return scale * (scaled - first - hat * second), jnp.sum(upstream * hat, axis=0)


def gelu(values):
    return jax.nn.gelu(values, approximate=True)


def gelu_back(values, upstream):
    return jax.vjp(gelu, values)[1](upstream)[0].astype(BF)


def softmax(scores):
    exponent = jnp.exp(scores - jnp.max(scores, axis=-1, keepdims=True))
    return exponent / jnp.sum(exponent, axis=-1, keepdims=True)


def softmax_back(soft, upstream):
    return (soft * (upstream - jnp.sum(upstream * soft, axis=-1, keepdims=True))).astype(BF)


def local(
    inputs,
    latent,
    gain_latent,
    gain_inputs,
    cross_query,
    cross_keys,
    cross_values,
    cross_output,
    cross_gain,
    cross_up,
    cross_down,
    self_gain,
    self_query,
    self_keys,
    self_values,
    self_output,
    self_mlp_gain,
    self_mlp_up,
    self_mlp_down,
    cotangent,
):
    cols = lax.axis_size("col")
    rows = lax.axis_size("row")
    place = lax.axis_index("col")
    wide = latent.shape[1] * cols
    block = latent.shape[1]
    lat_count = latent.shape[0] * rows
    head_size = wide // HEADS
    in_width = inputs.shape[1]
    images = inputs.shape[0] // M
    share = max(1, cols // images)
    assert images * share == cols
    here = lat_count // share
    groups = [[image * share + part for part in range(share)] for image in range(images)]
    cross_scale = wide ** (-0.5)
    self_scale = head_size ** (-0.5)

    by_row = (cross_up, self_query, self_keys, self_values, self_mlp_up)
    by_col = (cross_query, cross_output, cross_down, self_output, self_mlp_down)
    stack = jnp.stack([item.T for item in by_col] + list(by_row))
    count = stack.shape[0]
    deep = stack.shape[1]
    whole = lax.all_gather(stack, BOTH, axis=0, tiled=False)
    whole = whole.reshape(rows, cols, count, deep, block)
    whole = whole.transpose(2, 0, 3, 1, 4).reshape(count, wide, wide)
    t_query, t_output, t_down, t_self_output, t_self_down, up, s_query, s_keys, s_values, s_up = [
        whole[index] for index in range(count)
    ]
    lat_all = lax.all_gather(latent, BOTH, axis=0, tiled=False)
    lat_all = lat_all.reshape(rows, cols, -1, block).transpose(0, 2, 1, 3).reshape(lat_count, wide)
    pair = lax.all_gather(jnp.concatenate([cross_keys, cross_values]), "col", axis=1, tiled=True)
    c_keys, c_values = pair[:in_width], pair[in_width:]
    gains = lax.all_gather(
        jnp.stack([gain_latent, cross_gain, self_gain, self_mlp_gain]), "col", axis=1, tiled=True
    )
    g_lat, g_cross, g_self, g_mlp = [gains[index] for index in range(4)]
    grad_out_low = lax.all_to_all(cotangent, "col", split_axis=0, concat_axis=1, tiled=True)

    start = (place % share) * here
    lat = lax.dynamic_slice_in_dim(lat_all, start, here, axis=0).astype(F32)
    pixels = lax.dynamic_slice_in_dim(inputs, (place // share) * M, M, axis=0).astype(F32)

    lat_low, lat_hat, lat_scale = norm(lat, g_lat)
    queries = nt(lat_low, t_query).astype(BF)
    pix_low, pix_hat, pix_scale = norm(pixels, gain_inputs)
    key_rows = nn(pix_low, c_keys).astype(BF)
    values = nn(pix_low, c_values).astype(BF)
    soft = softmax(nt(queries, key_rows) * cross_scale)
    soft_low = soft.astype(BF)
    attended = nn(soft_low, values).astype(BF)
    state_one = lat + nt(attended, t_output)
    mlp_low, mlp_hat, mlp_scale = norm(state_one, g_cross)
    hidden = nn(mlp_low, up)
    active = gelu(hidden).astype(BF)
    state_two = state_one + nt(active, t_down)
    attn_low, attn_hat, attn_scale = norm(state_two, g_self)
    head_q = nn(attn_low, s_query).astype(BF)
    head_k = nn(attn_low, s_keys).astype(BF)
    head_v = nn(attn_low, s_values).astype(BF)
    if share > 1:
        head_k, head_v = [
            lax.all_gather(item, "col", axis_index_groups=groups, axis=0, tiled=True)
            for item in (head_k, head_v)
        ]

    def split(item):
        return item.reshape(item.shape[0], HEADS, head_size)

    def join(item):
        return item.astype(BF).reshape(item.shape[0], wide)

    def contract(form, left, right):
        return jnp.einsum(form, left, right, preferred_element_type=F32)

    hq, hk, hv = split(head_q), split(head_k), split(head_v)
    self_soft = softmax(contract("qhd,khd->hqk", hq, hk) * self_scale)
    self_soft_low = self_soft.astype(BF)
    self_att = join(contract("hqk,khd->qhd", self_soft_low, hv))
    state_three = state_two + nt(self_att, t_self_output)
    last_low, last_hat, last_scale = norm(state_three, g_mlp)
    hidden_two = nn(last_low, s_up)
    active_two = gelu(hidden_two).astype(BF)
    result = (state_three + nt(active_two, t_self_down)).astype(BF)
    result = lax.all_to_all(result, "col", split_axis=1, concat_axis=0, tiled=True)

    grad_self_down = tn(grad_out_low, active_two)
    dh2 = gelu_back(hidden_two, nn(grad_out_low, t_self_down))
    grad_self_up = tn(last_low, dh2)
    back, gain_mlp = norm_back(nt(dh2, s_up), g_mlp, last_hat, last_scale)
    g3 = grad_out_low.astype(F32) + back
    g3_low = g3.astype(BF)
    grad_self_output = tn(g3_low, self_att)
    d_att = split(nn(g3_low, t_self_output).astype(BF))
    d_self = softmax_back(self_soft, contract("qhd,khd->hqk", d_att, hv))
    dq = join(contract("hqk,khd->qhd", d_self, hk) * self_scale)
    dk = contract("hqk,qhd->khd", d_self, hq) * self_scale
    dvv = contract("hqk,qhd->khd", self_soft_low, d_att)
    dk, dvv = join(dk), join(dvv)
    if share > 1:
        dk, dvv = [
            lax.psum_scatter(
                item, "col", axis_index_groups=groups, scatter_dimension=0, tiled=True
            )
            for item in (dk, dvv)
        ]
    grad_query, grad_keys, grad_values = tn(attn_low, dq), tn(attn_low, dk), tn(attn_low, dvv)
    dy = nt(dq, s_query) + nt(dk, s_keys) + nt(dvv, s_values)
    back, gain_self = norm_back(dy, g_self, attn_hat, attn_scale)
    g2 = g3 + back
    g2_low = g2.astype(BF)
    grad_down = tn(g2_low, active)
    dh1 = gelu_back(hidden, nn(g2_low, t_down))
    grad_up = tn(mlp_low, dh1)
    back, gain_cross = norm_back(nt(dh1, up), g_cross, mlp_hat, mlp_scale)
    g1 = g2 + back
    g1_low = g1.astype(BF)
    grad_output = tn(g1_low, attended)
    d_attended = nn(g1_low, t_output).astype(BF)
    d_scores = softmax_back(soft, nt(d_attended, values))
    d_queries = (nn(d_scores, key_rows) * cross_scale).astype(BF)
    d_keys = (tn(d_scores, queries) * cross_scale).astype(BF)
    d_values = tn(soft_low, d_attended).astype(BF)
    grad_cross_query = tn(d_queries, lat_low)
    grad_pair = jnp.concatenate([tn(pix_low, d_keys), tn(pix_low, d_values)])
    d_pix = nt(d_keys, c_keys) + nt(d_values, c_values)
    grad_inputs, gain_pix = norm_back(d_pix, gain_inputs, pix_hat, pix_scale)
    if share > 1:
        grad_inputs = lax.psum_scatter(
            grad_inputs, "col", axis_index_groups=groups, scatter_dimension=0, tiled=True
        )
    back, gain_lat = norm_back(nn(d_queries, t_query), g_lat, lat_hat, lat_scale)
    grad_lat = g1 + back
    if share > 1:
        grad_lat = lax.dynamic_update_slice_in_dim(
            jnp.zeros((lat_count, wide), F32), grad_lat, start, axis=0
        )

    def reduce(item):
        item = lax.psum_scatter(item, "row", scatter_dimension=0, tiled=False)
        return lax.psum_scatter(item, "col", scatter_dimension=0, tiled=False).astype(F32)

    grads = jnp.stack(
        [
            item.astype(BF)
            for item in (
                grad_cross_query,
                grad_output,
                grad_down,
                grad_self_output,
                grad_self_down,
                grad_up,
                grad_query,
                grad_keys,
                grad_values,
                grad_self_up,
            )
        ]
    )
    grads = grads.reshape(count, rows, deep, cols, block).transpose(1, 3, 0, 2, 4)
    grads = reduce(grads)
    grad_lat = reduce(
        grad_lat.astype(BF).reshape(rows, -1, cols, block).transpose(0, 2, 1, 3)
    )
    grad_pair = lax.psum_scatter(
        grad_pair.astype(BF).reshape(-1, cols, block).transpose(1, 0, 2),
        "col",
        scatter_dimension=0,
        tiled=False,
    )
    grad_pair = lax.psum(grad_pair, "row").astype(F32)
    gain_all, gain_pix = lax.psum(
        (jnp.stack([gain_lat, gain_cross, gain_self, gain_mlp]), gain_pix), BOTH
    )
    gain_all = lax.dynamic_slice_in_dim(gain_all, place * block, block, axis=1)
    return (
        result,
        grad_inputs,
        grad_lat,
        gain_all[0],
        gain_pix,
        grads[0].T,
        grad_pair[:in_width],
        grad_pair[in_width:],
        grads[1].T,
        gain_all[1],
        grads[5],
        grads[2].T,
        gain_all[2],
        grads[6],
        grads[7],
        grads[8],
        grads[3].T,
        gain_all[3],
        grads[9],
        grads[4].T,
    )


def solution(mesh):
    rc, cr, c, cc = P("row", "col"), P("col", "row"), P("col"), P(None, "col")
    return jax.shard_map(
        local,
        mesh=mesh,
        in_specs=(
            P("row", None), rc, c, P(), cr, cc, cc, cr, c, rc, cr, c, rc, rc, rc, cr, c, rc, cr, rc,
        ),
        out_specs=(
            rc, P(BOTH, None), rc, c, P(), cr, cc, cc, cr, c, rc, cr, c, rc, rc, rc, cr, c, rc, cr,
        ),
        check_vma=False,
    )
```

time: 2890 us -> 826 us (0.29)
  waiting for transfers between devices: 2080 us -> 389 us
  blocking collectives: 321 us -> 88.3 us
  other arithmetic: 152 us -> 27.5 us
  matrix products: 240 us -> 124 us
  local copies, waits for them, and re-layouts: 60.7 us -> 154 us
    reduce_scatter x36 -> x5, waiting for transfers between devices: 916 us -> 201 us  [the longest x2 138 us: reduce(): item = lax.psum_scatter(item, 'row', scatter_dimension=0, tiled=False)]
    all_gather x32 -> x3, waiting for transfers between devices: 644 us -> 162 us  [the longest x1 121 us: local(): whole = lax.all_gather(stack, BOTH, axis=0, tiled=False)]
    psum x5 -> x1, waiting for transfers between devices: 365 us -> 24.2 us  [local(): grad_pair = lax.psum(grad_pair, 'row').astype(F32)]
    psum x15 -> x1, blocking collectives: 197 us -> 41.5 us  [local(): lax.psum((jnp.stack([gain_lat, gain_cross, gain_self, gain_mlp]), gain_pi...]
    unnamed x83 -> x9, waiting for transfers between devices: 156 us -> 1.48 us
    dot_general x189 -> x46, matrix products: 240 us -> 116 us  [the longest x14 39 us: tn(): lax.dot_general(left, right, (((0,), (0,)), ((), ())), preferred_element_...]
    all_gather x11 -> x1, blocking collectives: 113 us -> 46.8 us  [local(): lax.all_gather(jnp.stack([gain_latent, cross_gain, self_gain, self_mlp_ga...]
    convert_element_type x43 -> x8, other arithmetic: 61.7 us -> 8.65 us  [the longest x2 3.04 us: softmax_back(): (soft * (upstream - jnp.sum(upstream * soft, axis=-1, keepdims=True))).as...]
  transfers between devices with their start and end apart: 78 -> 11, of which waited for: 73 -> 6; matrix products, arithmetic and copies ran while one was open for 10% -> 14% of each run, Pallas kernels for 0% -> 0%
where the time goes in v1:
time: 826 us; the launch traced here: 815 us
  waiting for transfers between devices  389 us (47%)
  local copies, waits for them, and re-layouts  154 us (19%)
  matrix products  124 us (15%)
  blocking collectives  88.3 us (11%)
  other arithmetic  27.5 us (3%)
  between operations  15.5 us (2%)
  starting transfers between devices  11.5 us (1%)
    reduce_scatter x2, waiting for transfers between devices, reduce(): item = lax.psum_scatter(item, 'row', scatter_dimension=0, tiled=False)  138 us
    all_gather x1, waiting for transfers between devices, local(): whole = lax.all_gather(stack, BOTH, axis=0, tiled=False)  121 us
    reduce_scatter x2, waiting for transfers between devices, reduce(): lax.psum_scatter(item, 'col', scatter_dimension=0, tiled=False).astype(F32)  53.6 us
    unnamed x192, local copies, waits for them, and re-layouts  53.2 us
    all_gather x1, blocking collectives, local(): lax.all_gather(jnp.stack([gain_latent, cross_gain, self_gain, self_mlp_ga...  46.8 us
    all_gather x1, waiting for transfers between devices, local(): lat_all = lax.all_gather(latent, BOTH, axis=0, tiled=False)  41.6 us
    psum x1, blocking collectives, local(): lax.psum((jnp.stack([gain_lat, gain_cross, gain_self, gain_mlp]), gain_pi...  41.5 us
    dot_general x14, matrix products, tn(): lax.dot_general(left, right, (((0,), (0,)), ((), ())), preferred_element_...  39 us
  transfers between devices with their start and end apart: 11, of which 6 were waited for; matrix products, arithmetic and copies ran while one was open for 14% of the time, Pallas kernels for 0%

profile of v1, /device:TPU:0, one launch (start us, length us, event | category | flops | bytes accessed | tf_op | source)
XLA Modules:
  0.0 815.4 jit_solution(8326261063209987246)
XLA Ops:
  15.9 6.4 all-to-all-start.1
  22.3 46.8 %all_gather.20 = f32[4,1024]{1,0:T(4,128)S(1)} all-gather(f32[4,256]{1,0:T(4,128)S(1)} %pad_maximum_fusion.2), channel_id=1, replica_groups=mesh['row'=8,'col'=4] {'col'}, dimensions={1}, use_global_device_ids=true | all-gather | bytes 20480 | tf_op jit(solution)/shard_map/all_gather | solution.py:111
  73.9 4.4 fusion.166
  78.3 41.6 %all-gather.8.cloned.1.call-done = bf16[2048,256]{1,0:T(8,128)(2,1)} async-done(((bf16[64,256]{1,0:T(8,128)(2,1)}), bf16[2048,256]{1,0:T(8,128)(2,1)}) %all-gather.8.cloned.1.call-update) | async-done | bytes 1048592 | tf_op jit(solution)/shard_map/all_gather | solution.py:107
  126.0 7.4 multiply_reduce_fusion.14
  135.5 120.6 %all-gather.10.cloned.1.call-done = bf16[320,128,256]{2,1,0:T(8,128)(2,1)} async-done(((bf16[10,128,256]{2,1,0:T(8,128)(2,1)}), bf16[320,128,256]{2,1,0:T(8,128)(2,1)}) %all-gather.10.cloned.1.call-update) | async-done | bytes 20971536 | tf_op jit(solution)/shard_map/all_gather | solution.py:101
  256.1 30.8 %copy.120 = bf16[8,4,10,128,256]{3,0,4,1,2:T(8,128)(2,1)} copy(bf16[8,4,10,128,256]{4,3,2,1,0:T(8,128)(2,1)} %bitcast.339) | data formatting | bytes 41943040 | tf_op jit(solution)/shard_map/reshape | solution.py:102
  286.9 14.4 %fusion.177 = (bf16[1,8,128,4,256]{2,1,4,3,0:T(8,128)(2,1)}, bf16[1,8,128,4,256]{2,1,4,3,0:T(8,128)(2,1)}, bf16[1,8,128,4,256]{2,1,4,3,0:T(8,128)(2,1)}, bf16[1,...) fusion(bf16[10,8,128,4,256]{2,1,4,3,0:T(8,128)(2,1)} %bitcast.338), kind=kLoop, calls=%fused_computation.268 | loop fusion | bytes 41943040 | tf_op jit(solution)/shard_map/slice | solution.py:105
  306.2 5.8 online-softmax
  312.0 4.2 fusion.181
  336.8 7.5 fusion.183
  344.4 4.7 fusion.99
  365.6 5.3 fusion.102
  371.0 4.4 multiply_reduce_fusion
  441.5 4.6 stack.117
  449.0 4.7 stack.119
  461.2 4.6 stack.122
  468.7 4.7 stack.124
  513.0 9.4 %reduce-scatter.14.cloned.1.call-done = bf16[1,522,256]{2,1,0:T(8,128)(2,1)} async-done(((bf16[4,522,256]{2,1,0:T(8,128)(2,1)}), bf16[1,522,256]{2,1,0:T(8,128)(2,1)}) %reduce-scatter.14.cloned.1.call-update) | async-done | bytes 267280 | tf_op jit(solution)/shard_map/reduce_scatter | solution.py:242
  522.5 138.4 %reduce-scatter.10.cloned.1.call-done = bf16[1,4,10,128,256]{4,3,2,1,0:T(8,128)(2,1)} async-done(((bf16[8,4,10,128,256]{4,3,2,1,0:T(8,128)(2,1)}), bf16[1,4,10,128,256]{4,3,2,1,0:T(8,128)(2,1)}) %reduce-scatter.10.cloned.1.call-update) | async-done | bytes 2621456 | tf_op jit(solution)/shard_map/reduce_scatter | solution.py:217
  665.7 4.9 all-to-all-start
  676.0 41.5 %all-reduce = (f32[4,1024]{1,0:T(4,128)S(1)}, f32[261]{0:T(512)}) all-reduce(f32[4,1024]{1,0:T(4,128)S(1)} %pad_maximum_fusion.1, f32[261]{0:T(512)S(1)} %get-tuple-element.68), channel_id=1, replica_groups=mesh['row'=8,'col'=4] {'row','col'}, use_global_device_ids=true, to_apply=%region_32.33 | all-reduce | flops 4357 | bytes 34856 | tf_op jit(solution)/shard_map/psum | solution.py:249
  722.1 24.2 %all-reduce.3.cloned.1.call-done = bf16[522,256]{1,0:T(8,128)(2,1)} async-done(((bf16[522,256]{1,0:T(8,128)(2,1)}), bf16[522,256]{1,0:T(8,128)(2,1)}) %all-reduce.3.cloned.1.call-update) | async-done | bytes 267280 | tf_op jit(solution)/shard_map/psum | solution.py:248
  748.1 53.6 %reduce-scatter.12.cloned.1.call-done = bf16[1,10,128,256]{3,2,1,0:T(8,128)(2,1)} async-done(((bf16[4,10,128,256]{3,2,1,0:T(8,128)(2,1)}), bf16[1,10,128,256]{3,2,1,0:T(8,128)(2,1)}) %reduce-scatter.12.cloned.1.call-update) | async-done | bytes 655376 | tf_op jit(solution)/shard_map/reduce_scatter | solution.py:218
  (326 shorter events, 205.1 us)
Async XLA Ops:
  7.2 7.7 copy-start.48
  7.2 7.8 copy-start.49
  7.2 7.8 copy-start.50
  7.2 7.8 copy-start.51
  7.2 62.5 %all-gather.6.cloned.1.call-start = ((), (), s32[]{:S(2)}) async-start(), calls=%async_computation.7 | async-start | bytes 1351680 | tf_op jit(solution)/shard_map/all_gather | solution.py:109
  9.1 110.8 %all-gather.8.cloned.1.call-start = ((), (), s32[]{:S(2)}) async-start(), calls=%async_computation.14 | async-start | bytes 1081344 | tf_op jit(solution)/shard_map/all_gather | solution.py:107
  9.8 246.3 %all-gather.10.cloned.1.call-start = ((), (), s32[]{:S(2)}) async-start(), calls=%async_computation.15 | async-start | bytes 21626880 | tf_op jit(solution)/shard_map/all_gather | solution.py:101
  12.7 9.5 %copy-start.58 = (f32[256]{0:T(256)S(1)}, f32[256]{0:T(256)}, u32[]{:S(2)}) copy-start(f32[256]{0:T(256)} %param.36) | copy-start | bytes 3076
  12.7 9.5 %copy-start.59 = (f32[256]{0:T(256)S(1)}, f32[256]{0:T(256)}, u32[]{:S(2)}) copy-start(f32[256]{0:T(256)} %param.31) | copy-start | bytes 3076
  12.8 9.5 %copy-start.60 = (f32[256]{0:T(256)S(1)}, f32[256]{0:T(256)}, u32[]{:S(2)}) copy-start(f32[256]{0:T(256)} %param.28) | copy-start | bytes 3076
  12.8 9.5 %copy-start.61 = (f32[256]{0:T(256)S(1)}, f32[256]{0:T(256)}, u32[]{:S(2)}) copy-start(f32[256]{0:T(256)} %param.22) | copy-start | bytes 3076
  13.7 55.4 %copy-start.41 = (bf16[4096,261]{0,1:T(8,128)(2,1)S(1)}, bf16[4096,261]{0,1:T(8,128)(2,1)}, u32[]{:S(2)}) copy-start(bf16[4096,261]{0,1:T(8,128)(2,1)} %param.20) | copy-start | bytes 6414340
  15.9 53.6 %all-to-all-start.1 = ((bf16[4,512,256]{2,1,0:T(8,128)(2,1)}), bf16[4,512,256]{2,1,0:T(8,128)(2,1)S(1)}, u32[]{:S(2)}, u32[]{:S(2)}) async-start(bf16[4,512,256]{2,1,0:T(8,128)(2,1)} %bitcast.381), calls=%async_computation.1 | async-start | bytes 2097152 | tf_op jit(solution)/shard_map/all_to_all | solution.py:115
  22.3 47.4 %copy-start.56 = (f32[261]{0:T(512)S(1)}, f32[261]{0:T(512)}, u32[]{:S(2)}) copy-start(f32[261]{0:T(512)} %param.23) | copy-start | bytes 3136
  22.3 490.0 %reduce-scatter.6.cloned.1.call-start = ((), (), s32[]{:S(2)}) async-start(), calls=%async_computation.8 | async-start | bytes 1179648 | tf_op jit(solution)/shard_map/reduce_scatter | solution.py:217
  350.7 8.1 copy-start.17
  365.6 9.8 %slice-start = ((s8[8388608]{0:T(1024)(128)(4,1)}), s8[4194304]{0:T(1024)(128)(4,1)S(1)}, s32[]{:S(2)}) async-start(s8[8388608]{0:T(1024)(128)(4,1)} %bitcast.344), calls=%async_computation.16 | async-start | bytes 8388608
  441.5 81.0 %reduce-scatter.14.cloned.1.call-start = ((), (), s32[]{:S(2)}) async-start(), calls=%async_computation.12 | async-start | bytes 1351680 | tf_op jit(solution)/shard_map/reduce_scatter | solution.py:242
  496.2 164.7 %reduce-scatter.10.cloned.1.call-start = ((), (), s32[]{:S(2)}) async-start(), calls=%async_computation.10 | async-start | bytes 23592960 | tf_op jit(solution)/shard_map/reduce_scatter | solution.py:217
  512.2 148.7 %copy-start.19 = (f32[512,1024]{1,0:T(8,128)S(1)}, f32[512,1024]{1,0:T(8,128)}, u32[]{:S(2)}) copy-start(f32[512,1024]{1,0:T(8,128)} %copy-done.17) | copy-start | bytes 6291460
  512.2 208.5 %reduce-scatter.8.cloned.1.call-start = ((), (), s32[]{:S(2)}) async-start(), calls=%async_computation.9 | async-start | bytes 163840 | tf_op jit(solution)/shard_map/reduce_scatter | solution.py:218
  513.0 233.3 %all-reduce.3.cloned.1.call-start = ((), (), s32[]{:S(2)}) async-start(), calls=%async_computation.13 | async-start | bytes 540672 | tf_op jit(solution)/shard_map/psum | solution.py:248
  522.5 279.2 %reduce-scatter.12.cloned.1.call-start = ((), (), s32[]{:S(2)}) async-start(), calls=%async_computation.11 | async-start | bytes 3276800 | tf_op jit(solution)/shard_map/reduce_scatter | solution.py:218
  665.7 55.0 %all-to-all-start = ((bf16[512,4,256]{2,0,1:T(8,128)(2,1)}), bf16[512,4,256]{2,0,1:T(8,128)(2,1)S(1)}, u32[]{:S(2)}, u32[]{:S(2)}) async-start(bf16[512,4,256]{2,0,1:T(8,128)(2,1)} %bitcast.336), calls=%async_computation | async-start | bytes 2097152 | tf_op jit(solution)/shard_map/all_to_all | solution.py:162
  (67 other events, 184.4 us)
Sparse Core Ops, SparseCore 0:
  10.2 51.7 all-gather.5
  65.0 54.8 all-gather.7
  123.3 132.7 all-gather.9
  441.6 34.1 reduce-scatter.5
  496.3 26.0 reduce-scatter.13
  525.9 134.9 reduce-scatter.9
  663.1 20.9 reduce-scatter.7
  687.2 58.9 all-reduce.2
  748.6 53.0 reduce-scatter.11
